TPU v7x, 256 devices: a whole 4x4x8 slice. The times are simulated.
256 devices in a mesh: dp: 32 (over x, z), mp: 8 (over y, core).
Axes of the slice: x: 4, y: 4, z: 8, core: 2. Of those that a mesh axis runs over, the one named last changes fastest.
Arguments:
- residual_in: bfloat16 [8192, 5120], P('dp', 'mp'), may hold values from -6 to 6
- queries_in: bfloat16 [8192, 5120], P('dp', 'mp'), may hold values from -360 to 360
- key_values: bfloat16 [2, 8192, 1024], P(None, 'dp', 'mp'), may hold values from -6 to 6
- request_ids: int32 [8192], P('dp'), may hold values from 0 to 8191, as said below
- deal_order: int32 [32], replicated, may hold values from 0 to 31, each once
- page_table: int32 [512], P('dp'), may hold values from 0 to 511, as said below
- out_proj: bfloat16 [5120, 5120], P('dp', 'mp'), may hold values from -0.078125 to 0.078125
- norm_gain: bfloat16 [5120], P('mp'), may hold values from 0.099609375 to 1.8984375
- gate_up: bfloat16 [5120, 2, 16384], P('mp', None, 'dp'), may hold values from -0.078125 to 0.078125
Outputs:
- mlp_hidden: bfloat16 [8192, 16384], P('mp', 'dp')
- kv_cache: bfloat16 [512, 2, 16, 1024], P('dp', None, None, 'mp')
- residual_out: bfloat16 [8192, 5120], P('dp', 'mp')
Inputs may be any that keep to these rules, and one draw needn't show every extreme that they name: `request_ids`: each request lies whole inside one aligned block of 256 packed tokens, which holds one to three requests of 32 tokens or more; its id is the index of its first token. `page_table`: each aligned block of 16 entries is a permutation of that block's own page numbers.
All inputs are finite; a program needn't handle non-finite values.
Results may differ from a plain program's by a relative error of at most 0.02.
Values may be sent and summed in bfloat16 or wider, within the bound.
No kernel may reach another device: no remote copies, remote signals or barrier semaphores. Data moves between devices by JAX's collectives and lax.ppermute only.
A program may use at most 128 MiB of HBM per device.

v0:
```python
import jax
import jax.numpy as jnp
from jax import lax
from jax.sharding import PartitionSpec as P

D = 5120
HD = 128
epsilon = 1e-06


def attend(queries_in, key_values, request_ids):
    tok_rows = queries_in.shape[0]
    q_heads = queries_in.shape[1] // HD
    kv_heads = key_values.shape[2] // HD
    group = q_heads // kv_heads
    queries = queries_in.reshape(tok_rows, kv_heads, group, HD)
    keys = key_values[0].reshape(tok_rows, kv_heads, HD)
    values = key_values[1].reshape(tok_rows, kv_heads, HD)
    scores = jnp.einsum(
        "qhgd,khd->hgqk", queries, keys, preferred_element_type=jnp.float32
    ) * HD ** (-0.5)
    places = jnp.arange(tok_rows, dtype=jnp.int32)
    allowed = (request_ids[:, None] == request_ids[None, :]) & (places[None, :] <= places[:, None])
    scores = jnp.where(allowed, scores, -1e30)
    row_max = jnp.max(scores, axis=-1, keepdims=True)
    lifted = jnp.exp(scores - row_max)
    weights = (lifted / jnp.sum(lifted, axis=-1, keepdims=True)).astype(jnp.bfloat16)
    mixed = jnp.einsum("hgqk,khd->qhgd", weights, values, preferred_element_type=jnp.float32)
    return mixed.astype(jnp.bfloat16).reshape(tok_rows, q_heads * HD)


def shards(
    residual_in,
    queries_in,
    key_values,
    request_ids,
    deal_order,
    page_table,
    out_proj,
    norm_gain,
    gate_up,
):
    tok_rows = residual_in.shape[0]
    local_width = residual_in.shape[1]
    pages_here = page_table.shape[0]
    page_rows = tok_rows // pages_here
    channels = key_values.shape[2]
    pages = key_values.reshape(2, pages_here, page_rows, channels).transpose(1, 0, 2, 3)
    kv_cache = jnp.zeros_like(pages).at[page_table % pages_here].set(pages)
    attended = attend(queries_in, key_values, request_ids)
    all_heads = lax.all_gather(attended, "mp", axis=1, tiled=True)
    projected = jnp.dot(
        all_heads,
        lax.all_gather(out_proj, "dp", axis=0, tiled=True),
        preferred_element_type=jnp.float32,
    )
    resid = residual_in.astype(jnp.float32) + projected
    square_sums = lax.psum(jnp.sum(resid * resid, axis=1), "mp")
    mean_square = square_sums / D
    normed = (
        resid * lax.rsqrt(mean_square + epsilon)[:, None] * norm_gain.astype(jnp.float32)
    ).astype(jnp.bfloat16)
    every_row = lax.all_gather(normed, "dp", axis=0, tiled=True)
    dp_count = lax.axis_size("dp")
    packed_blocks = every_row.reshape(dp_count, tok_rows, local_width)
    hidden_here = gate_up.shape[2]
    flat_weights = gate_up.reshape(local_width, 2 * hidden_here)
    own_rows = every_row.shape[0] // lax.axis_size("mp")
    picked = jnp.take(packed_blocks, deal_order, axis=0).reshape(
        own_rows * lax.axis_size("mp"), local_width
    )
    partial_sum = jnp.dot(picked, flat_weights, preferred_element_type=jnp.float32).astype(
        jnp.bfloat16
    )
    partial_sum = lax.optimization_barrier(partial_sum)
    summed = lax.psum_scatter(
        partial_sum.astype(jnp.float32).astype(jnp.bfloat16), "mp", scatter_dimension=0, tiled=True
    ).astype(jnp.float32)
    mlp_hidden = (jax.nn.silu(summed[:, :hidden_here]) * summed[:, hidden_here:]).astype(
        jnp.bfloat16
    )
    return (mlp_hidden, kv_cache, resid.astype(jnp.bfloat16))


def solution(mesh):
    in_specs = (
        P("dp", "mp"),
        P("dp", "mp"),
        P(None, "dp", "mp"),
        P("dp"),
        P(),
        P("dp"),
        P("dp", "mp"),
        P("mp"),
        P("mp", None, "dp"),
    )
    out_specs = (P("mp", "dp"), P("dp", None, None, "mp"), P("dp", "mp"))
    return jax.shard_map(shards, mesh=mesh, in_specs=in_specs, out_specs=out_specs, check_vma=False)
```

profile of v0, /device:TPU:1, one launch (start us, length us, event | category | flops | bytes accessed | tf_op | source)
XLA Modules:
  0.0 402.9 jit_solution(12429837756996770780)
XLA Ops:
  7.2 0.0 copy-start.3
  7.2 0.0 all-gather.4.cloned.1.call-start
  7.2 1.2 copy.16
  8.4 0.9 fusion.5
  9.3 1.2 fusion.12
  10.5 0.2 fusion.3
  10.7 0.0 copy-start.4
  10.7 0.0 copy-start.2
  10.7 1.1 convolution_convert_fusion.1
  11.8 0.0 all-gather.4.cloned.1.call-update
  11.8 0.0 all-gather.6.cloned.1.call-start
  11.9 0.7 all-gather.6.cloned.1.call-update
  12.6 0.0 all-gather.8.cloned.1.call-start
  12.6 32.1 %all-gather.4.cloned.1.call-done = bf16[256,5120]{0,1:T(8,128)(2,1)} async-done(((bf16[256,640]{0,1:T(8,128)(2,1)}), bf16[256,5120]{0,1:T(8,128)(2,1)}) %all-gather.4.cloned.1.call-update) | async-done | bytes 2621456 | tf_op jit(solution)/shard_map/all_gather | solution.py:51
  44.7 91.6 %all-gather.6.cloned.1.call-done = bf16[5120,640]{1,0:T(8,128)(2,1)} async-done(((bf16[160,640]{1,0:T(8,128)(2,1)}), bf16[5120,640]{1,0:T(8,128)(2,1)}) %all-gather.6.cloned.1.call-update) | async-done | bytes 6553616 | tf_op jit(solution)/shard_map/all_gather | solution.py:54
  136.3 6.0 %multiply_reduce_fusion = (f32[256]{0:T(256)S(1)}, f32[256,640]{1,0:T(8,128)S(1)}) fusion(bf16[256,5120]{0,1:T(8,128)(2,1)} %all-gather.4.cloned.1.call-done, bf16[5120,640]{1,0:T(8,128)(2,1)} %all-gather.6.cloned.1.call-done, bf16[256,640]{1,0:T(8,128)(2,1)S(1)} %copy-done.2), kind=kOutput, calls=%fused_computation.16 | convolution fusion | flops 1678376704 | bytes 10159104 | tf_op jit(solution)/shard_map/dot_general | solution.py:52
  142.3 13.1 %psum.7 = f32[256]{0:T(256)S(1)} all-reduce(f32[256]{0:T(256)S(1)} %get-tuple-element.7), channel_id=1, replica_groups=mesh['dp'=32,'mp'=8] {'mp'}, use_global_device_ids=true, to_apply=%region_3.4 | all-reduce | flops 256 | bytes 2048 | tf_op jit(solution)/shard_map/psum | solution.py:58
  155.4 1.0 fusion.11
  156.4 0.0 all-gather.8.cloned.1.call-update
  156.4 0.0 reduce-scatter.2.cloned.1.call-start
  156.4 0.3 copy.24
  156.8 103.8 %all-gather.8.cloned.1.call-done = bf16[8192,640]{1,0:T(8,128)(2,1)} async-done(((bf16[256,640]{1,0:T(8,128)(2,1)}), bf16[8192,640]{1,0:T(8,128)(2,1)}) %all-gather.8.cloned.1.call-update) | async-done | bytes 10485776 | tf_op jit(solution)/shard_map/all_gather | solution.py:63
  260.6 10.2 %gather_fusion = bf16[32,256,640]{2,1,0:T(8,128)(2,1)} fusion(bf16[32,256,640]{2,1,0:T(8,128)(2,1)} %bitcast.41, s32[1024]{0:T(1024)S(1)} %pad_clamp_fusion), kind=kCustom, calls=%fused_computation | custom fusion | bytes 20971648 | tf_op jit(solution)/shard_map/jit(_take)/gather | solution.py:69
  270.8 10.2 %broadcast_select_fusion = bf16[32,256,640]{2,1,0:T(8,128)(2,1)} fusion(bf16[32,256,640]{2,1,0:T(8,128)(2,1)} %gather_fusion, pred[32]{0:T(512)(128)(4,1)S(1)} %compare_and_fusion), kind=kLoop, calls=%fused_computation.3 | loop fusion | flops 5242880 | bytes 20971552 | tf_op jit(solution)/shard_map/jit(_take)/select_n | solution.py:69
  281.0 19.9 %convolution_convert_fusion = bf16[8192,1024]{1,0:T(8,128)(2,1)} fusion(bf16[8192,640]{1,0:T(8,128)(2,1)} %bitcast.42, bf16[640,1024]{1,0:T(8,128)(2,1)S(1)} %bitcast.45), kind=kOutput, calls=%fused_computation.2 | convolution fusion | flops 10745806848 | bytes 28573696 | tf_op jit(solution)/shard_map/dot_general | solution.py:72
  300.9 0.0 reduce-scatter.2.cloned.1.call-update
  300.9 0.6 copy-done.6
  301.6 1.0 scatter_fusion
  302.6 0.0 copy-start.1
  302.6 90.1 %reduce-scatter.2.cloned.1.call-done = bf16[1024,1024]{1,0:T(8,128)(2,1)} async-done(((bf16[8192,1024]{1,0:T(8,128)(2,1)}), bf16[1024,1024]{1,0:T(8,128)(2,1)}) %reduce-scatter.2.cloned.1.call-update) | async-done | bytes 2097168 | tf_op jit(solution)/shard_map/reduce_scatter | solution.py:76
  392.7 2.0 convert_element_type.47
  394.7 1.7 fusion
  (17 shorter events, 0.1 us)
Async XLA Ops:
  7.2 3.5 copy-start.3
  7.2 37.5 %all-gather.4.cloned.1.call-start = ((), (), s32[]{:S(2)}) async-start(), calls=%async_computation.1 | async-start | bytes 2949120 | tf_op jit(solution)/shard_map/all_gather | solution.py:51
  10.7 1.9 copy-start.4
  10.7 125.7 %copy-start.2 = (bf16[256,640]{1,0:T(8,128)(2,1)S(1)}, bf16[256,640]{1,0:T(8,128)(2,1)}, u32[]{:S(2)}) copy-start(bf16[256,640]{1,0:T(8,128)(2,1)} %param.9) | copy-start | bytes 983044
  11.8 124.5 %all-gather.6.cloned.1.call-start = ((), (), s32[]{:S(2)}) async-start(), calls=%async_computation.2 | async-start | bytes 6758400 | tf_op jit(solution)/shard_map/all_gather | solution.py:54
  12.6 248.0 %all-gather.8.cloned.1.call-start = ((), (), s32[]{:S(2)}) async-start(), calls=%async_computation.3 | async-start | bytes 10813440 | tf_op jit(solution)/shard_map/all_gather | solution.py:63
  142.3 14.1 %copy-start = (bf16[640,2,512]{2,1,0:T(2,128)(2,1)S(1)}, bf16[640,2,512]{2,1,0:T(2,128)(2,1)}, u32[]{:S(2)}) copy-start(bf16[640,2,512]{2,1,0:T(2,128)(2,1)} %param.17) | copy-start | bytes 3932164
  155.4 1.4 copy-start.5
  156.4 236.3 %reduce-scatter.2.cloned.1.call-start = ((), (), s32[]{:S(2)}) async-start(), calls=%async_computation.4 | async-start | bytes 18874368 | tf_op jit(solution)/shard_map/reduce_scatter | solution.py:76
  300.9 0.7 copy-start.6
  302.6 92.1 %copy-start.1 = (bf16[16,2,16,128]{3,2,1,0:T(8,128)(2,1)}, bf16[16,2,16,128]{3,2,1,0:T(8,128)(2,1)S(1)}, u32[]{:S(2)}) copy-start(bf16[16,2,16,128]{3,2,1,0:T(8,128)(2,1)S(1)} %scatter_fusion) | copy-start | bytes 393220
Sparse Core Ops, SparseCore 0:
  11.9 32.7 all-gather.3
  47.3 88.9 all-gather.5
  156.5 104.0 all-gather.7
  301.0 91.6 reduce-scatter.1
where the time goes:
time: 403 us
  waiting for transfers between devices  318 us (79%)
  matrix products  28.2 us (7%)
  other arithmetic  16 us (4%)
  between operations  13.9 us (3%)
  local copies, waits for them, and re-layouts  13.4 us (3%)
  blocking collectives  13.1 us (3%)
    all_gather x1, waiting for transfers between devices, shards(): every_row = lax.all_gather(normed, 'dp', axis=0, tiled=True)  104 us
    all_gather x1, waiting for transfers between devices, shards(): lax.all_gather(out_proj, 'dp', axis=0, tiled=True)  91.6 us
    reduce_scatter x1, waiting for transfers between devices, shards(): lax.psum_scatter(partial_sum.astype(jnp.float32).astype(jnp.bfloat16), 'm...  90.1 us
    all_gather x1, waiting for transfers between devices, shards(): all_heads = lax.all_gather(attended, 'mp', axis=1, tiled=True)  32.1 us
    dot_general x1, matrix products, shards(): jnp.dot(picked, flat_weights, preferred_element_type=jnp.float32)  19.9 us
    psum x1, blocking collectives, shards(): square_sums = lax.psum(jnp.sum(resid * resid, axis=1), 'mp')  13.1 us
    select_n x2, other arithmetic, shards(): jnp.take(packed_blocks, deal_order, axis=0)  10.2 us
    gather x1, local copies, waits for them, and re-layouts, shards(): jnp.take(packed_blocks, deal_order, axis=0)  10.2 us
  transfers between devices with their start and end apart: 4, of which 4 were waited for; matrix products, arithmetic and copies ran while one was open for 0% of the time, Pallas kernels for 0%

commit v1 on v0

--- a/solution.py
+++ b/solution.py
@@ -48,7 +48,16 @@
     pages = key_values.reshape(2, pages_here, page_rows, channels).transpose(1, 0, 2, 3)
     kv_cache = jnp.zeros_like(pages).at[page_table % pages_here].set(pages)
     attended = attend(queries_in, key_values, request_ids)
-    all_heads = lax.all_gather(attended, "mp", axis=1, tiled=True)
+    ways = lax.axis_size("mp")
+    up = [(d, (d + 1) % ways) for d in range(ways)]
+    down = [(d, (d - 1) % ways) for d in range(ways)]
+    earlier, later = ([attended], [attended])
+    for _ in range(ways // 2):
+        earlier.append(lax.ppermute(earlier[-1], "mp", up))
+    for _ in range((ways - 1) // 2):
+        later.append(lax.ppermute(later[-1], "mp", down))
+    line = jnp.concatenate([*earlier[::-1], *later[1:]], axis=1)
+    all_heads = jnp.roll(line, (lax.axis_index("mp") - ways // 2) * attended.shape[1], axis=1)
     projected = jnp.dot(
         all_heads,
         lax.all_gather(out_proj, "dp", axis=0, tiled=True),

time: 403 us -> 370 us (0.918)
  waiting for transfers between devices: 318 us -> 255 us
  starting transfers between devices: 0.16 us -> 18.3 us
  local copies, waits for them, and re-layouts: 13.4 us -> 25.7 us
    all_gather x1, waiting for transfers between devices: 91.6 us -> 51.1 us  [shards(): lax.all_gather(out_proj, 'dp', axis=0, tiled=True)]
    all_gather x1 -> x0, waiting for transfers between devices: 32.1 us -> none  [shards(): all_heads = lax.all_gather(attended, 'mp', axis=1, tiled=True)]
    ppermute x0 -> x7, starting transfers between devices: none -> 18.2 us  [the longest x4 10.1 us: shards(): earlier.append(lax.ppermute(earlier[-1], 'mp', up))]
    unnamed x16 -> x31, local copies, waits for them, and re-layouts: 2.13 us -> 13.7 us
    ppermute x0 -> x7, waiting for transfers between devices: none -> 9.28 us  [the longest x4 8.3 us: shards(): earlier.append(lax.ppermute(earlier[-1], 'mp', up))]
  transfers between devices with their start and end apart: 4 -> 10, of which waited for: 4 -> 9; matrix products, arithmetic and copies ran while one was open for 0% -> 5% of each run, Pallas kernels for 0% -> 0%
where the time goes in v1:
time: 370 us
  waiting for transfers between devices  255 us (69%)
  matrix products  28.3 us (8%)
  local copies, waits for them, and re-layouts  25.7 us (7%)
  starting transfers between devices  18.3 us (5%)
  other arithmetic  15.9 us (4%)
  between operations  13.9 us (4%)
  blocking collectives  12.9 us (3%)
    all_gather x1, waiting for transfers between devices, shards(): every_row = lax.all_gather(normed, 'dp', axis=0, tiled=True)  104 us
    reduce_scatter x1, waiting for transfers between devices, shards(): lax.psum_scatter(partial_sum.astype(jnp.float32).astype(jnp.bfloat16), 'm...  89.8 us
    all_gather x1, waiting for transfers between devices, shards(): lax.all_gather(out_proj, 'dp', axis=0, tiled=True)  51.1 us
    dot_general x1, matrix products, shards(): jnp.dot(picked, flat_weights, preferred_element_type=jnp.float32)  19.9 us
    unnamed x31, local copies, waits for them, and re-layouts  13.7 us
    psum x1, blocking collectives, shards(): square_sums = lax.psum(jnp.sum(resid * resid, axis=1), 'mp')  12.9 us
    gather x1, local copies, waits for them, and re-layouts, shards(): jnp.take(packed_blocks, deal_order, axis=0)  10.2 us
    select_n x2, other arithmetic, shards(): jnp.take(packed_blocks, deal_order, axis=0)  10.1 us
  transfers between devices with their start and end apart: 10, of which 9 were waited for; matrix products, arithmetic and copies ran while one was open for 5% of the time, Pallas kernels for 0%

profile of v1, /device:TPU:1, one launch (start us, length us, event | category | flops | bytes accessed | tf_op | source)
XLA Modules:
  0.0 369.6 jit_solution(2981905237068109284)
XLA Ops:
  8.0 1.1 copy.16
  9.1 0.9 fusion.10
  10.0 1.2 fusion.18
  11.4 1.2 convolution_convert_fusion.1
  12.6 2.7 collective-permute-start
  15.3 4.0 %collective-permute-done = bf16[256,640]{0,1:T(8,128)(2,1)S(1)} collective-permute-done((bf16[256,640]{0,1:T(8,128)(2,1)S(1)}, bf16[256,640]{0,1:T(8,128)(2,1)S(1)}, u32[]{:S(2)}, u32[]{:S(2)}) %collective-permute-start) | collective-permute-done | bytes 327712 | tf_op jit(solution)/shard_map/ppermute | solution.py:56
  19.3 2.5 collective-permute-start.1
  21.8 1.7 collective-permute-start.4
  23.5 2.3 collective-permute-done.1
  25.8 2.5 collective-permute-start.2
  28.6 2.7 collective-permute-start.5
  31.2 1.1 collective-permute-done.2
  32.3 2.4 collective-permute-start.3
  35.5 3.7 %collective-permute-start.6 = (bf16[256,640]{0,1:T(8,128)(2,1)S(1)}, bf16[256,640]{0,1:T(8,128)(2,1)S(1)}, u32[]{:S(2)}, u32[]{:S(2)}) collective-permute-start(bf16[256,640]{0,1:T(8,128)(2,1)S(1)} %collective-permute-done.5), channel_id=1, source_target_pairs={{0,7},{1,0},{2,1},{3,2},{4,3},{5,4},{6,5},{7,6},{8,15},{9,8},{10,9... | collective-permute-start | bytes 983048 | tf_op jit(solution)/shard_map/ppermute | solution.py:58
  39.2 0.9 collective-permute-done.3
  40.8 0.8 constant_dynamic-update-slice_fusion.14
  43.8 0.8 constant_dynamic-update-slice_fusion.10
  45.3 0.8 constant_dynamic-update-slice_fusion.8
  49.1 0.8 constant_dynamic-update-slice_fusion.3
  52.1 51.1 %all-gather.3.cloned.1.call-done = bf16[5120,640]{1,0:T(8,128)(2,1)} async-done(((bf16[160,640]{1,0:T(8,128)(2,1)}), bf16[5120,640]{1,0:T(8,128)(2,1)}) %all-gather.3.cloned.1.call-update) | async-done | bytes 6553616 | tf_op jit(solution)/shard_map/all_gather | solution.py:63
  103.2 6.0 %multiply_reduce_fusion = (f32[256]{0:T(256)S(1)}, f32[256,640]{1,0:T(8,128)S(1)}) fusion(bf16[5120,640]{1,0:T(8,128)(2,1)} %all-gather.3.cloned.1.call-done, bf16[256,10240]{0,1:T(8,128)(2,1)} %constant_dynamic-update-slice_fusion, s32[]{:T(128)S(6)} %select_n.48, bf16[256,640]{1,0:T(8,128)(2,1)S(1)} %copy-done.2), kind=kOutput, calls=%fused_computation.18 | convolution fusion | flops 1678376704 | bytes 10159108 | tf_op jit(solution)/shard_map/dot_general | solution.py:61
  109.2 12.9 %psum.7 = f32[256]{0:T(256)S(1)} all-reduce(f32[256]{0:T(256)S(1)} %get-tuple-element.7), channel_id=1, replica_groups=mesh['dp'=32,'mp'=8] {'mp'}, use_global_device_ids=true, to_apply=%region_3.4 | all-reduce | flops 256 | bytes 2048 | tf_op jit(solution)/shard_map/psum | solution.py:67
  122.1 1.0 fusion.17
  123.5 103.8 %all-gather.5.cloned.1.call-done = bf16[8192,640]{1,0:T(8,128)(2,1)} async-done(((bf16[256,640]{1,0:T(8,128)(2,1)}), bf16[8192,640]{1,0:T(8,128)(2,1)}) %all-gather.5.cloned.1.call-update) | async-done | bytes 10485776 | tf_op jit(solution)/shard_map/all_gather | solution.py:72
  227.3 10.2 %gather_fusion = bf16[32,256,640]{2,1,0:T(8,128)(2,1)} fusion(bf16[32,256,640]{2,1,0:T(8,128)(2,1)} %bitcast.40, s32[1024]{0:T(1024)S(1)} %pad_clamp_fusion), kind=kCustom, calls=%fused_computation | custom fusion | bytes 20971648 | tf_op jit(solution)/shard_map/jit(_take)/gather | solution.py:78
  237.5 10.1 %broadcast_select_fusion = bf16[32,256,640]{2,1,0:T(8,128)(2,1)} fusion(bf16[32,256,640]{2,1,0:T(8,128)(2,1)} %gather_fusion, pred[32]{0:T(512)(128)(4,1)S(1)} %compare_and_fusion), kind=kLoop, calls=%fused_computation.3 | loop fusion | flops 5242880 | bytes 20971552 | tf_op jit(solution)/shard_map/jit(_take)/select_n | solution.py:78
  247.7 19.9 %convolution_convert_fusion = bf16[8192,1024]{1,0:T(8,128)(2,1)} fusion(bf16[8192,640]{1,0:T(8,128)(2,1)} %bitcast.41, bf16[640,1024]{1,0:T(8,128)(2,1)S(1)} %bitcast.44), kind=kOutput, calls=%fused_computation.2 | convolution fusion | flops 10745806848 | bytes 28573696 | tf_op jit(solution)/shard_map/dot_general | solution.py:81
  267.6 0.9 copy-done.3
  268.6 1.0 scatter_fusion
  269.6 89.8 %reduce-scatter.2.cloned.1.call-done = bf16[1024,1024]{1,0:T(8,128)(2,1)} async-done(((bf16[8192,1024]{1,0:T(8,128)(2,1)}), bf16[1024,1024]{1,0:T(8,128)(2,1)}) %reduce-scatter.2.cloned.1.call-update) | async-done | bytes 2097168 | tf_op jit(solution)/shard_map/reduce_scatter | solution.py:85
  359.4 2.0 convert_element_type.47
  361.4 1.7 fusion.2
  (44 shorter events, 11.4 us)
Async XLA Ops:
  7.2 27.6 %copy-start.4 = (bf16[640]{0:T(1024)(128)(2,1)S(1)}, bf16[640]{0:T(1024)(128)(2,1)}, u32[]{:S(2)}) copy-start(bf16[640]{0:T(1024)(128)(2,1)} %param.16) | copy-start | bytes 3844
  7.2 96.0 %all-gather.3.cloned.1.call-start = ((), (), s32[]{:S(2)}) async-start(), calls=%async_computation.1 | async-start | bytes 6758400 | tf_op jit(solution)/shard_map/all_gather | solution.py:63
  7.9 219.4 %all-gather.5.cloned.1.call-start = ((), (), s32[]{:S(2)}) async-start(), calls=%async_computation.2 | async-start | bytes 10813440 | tf_op jit(solution)/shard_map/all_gather | solution.py:72
  12.6 6.7 %collective-permute-start = (bf16[256,640]{0,1:T(8,128)(2,1)S(1)}, bf16[256,640]{0,1:T(8,128)(2,1)S(1)}, u32[]{:S(2)}, u32[]{:S(2)}) collective-permute-start(bf16[256,640]{0,1:T(8,128)(2,1)S(1)} %bitcast.45), channel_id=1, source_target_pairs={{0,1},{1,2},{2,3},{3,4},{4,5},{5,6},{6,7},{7,0},{8,9},{9,10},{10,1... | collective-permute-start | bytes 983048 | tf_op jit(solution)/shard_map/ppermute | solution.py:56
  19.3 6.5 %collective-permute-start.1 = (bf16[256,640]{0,1:T(8,128)(2,1)S(1)}, bf16[256,640]{0,1:T(8,128)(2,1)S(1)}, u32[]{:S(2)}, u32[]{:S(2)}) collective-permute-start(bf16[256,640]{0,1:T(8,128)(2,1)S(1)} %collective-permute-done), channel_id=1, source_target_pairs={{0,1},{1,2},{2,3},{3,4},{4,5},{5,6},{6,7},{7,0},{8,9},{9,10},{10,1... | collective-permute-start | bytes 983048 | tf_op jit(solution)/shard_map/ppermute | solution.py:56
  21.8 6.8 %collective-permute-start.4 = (bf16[256,640]{0,1:T(8,128)(2,1)S(1)}, bf16[256,640]{0,1:T(8,128)(2,1)S(1)}, u32[]{:S(2)}, u32[]{:S(2)}) collective-permute-start(bf16[256,640]{0,1:T(8,128)(2,1)S(1)} %bitcast.46), channel_id=1, source_target_pairs={{0,7},{1,0},{2,1},{3,2},{4,3},{5,4},{6,5},{7,6},{8,15},{9,8},{10,9... | collective-permute-start | bytes 983048 | tf_op jit(solution)/shard_map/ppermute | solution.py:58
  25.8 6.5 %collective-permute-start.2 = (bf16[256,640]{0,1:T(8,128)(2,1)S(1)}, bf16[256,640]{0,1:T(8,128)(2,1)S(1)}, u32[]{:S(2)}, u32[]{:S(2)}) collective-permute-start(bf16[256,640]{0,1:T(8,128)(2,1)S(1)} %collective-permute-done.1), channel_id=1, source_target_pairs={{0,1},{1,2},{2,3},{3,4},{4,5},{5,6},{6,7},{7,0},{8,9},{9,10},{10,1... | collective-permute-start | bytes 983048 | tf_op jit(solution)/shard_map/ppermute | solution.py:56
  28.6 6.9 %collective-permute-start.5 = (bf16[256,640]{0,1:T(8,128)(2,1)S(1)}, bf16[256,640]{0,1:T(8,128)(2,1)S(1)}, u32[]{:S(2)}, u32[]{:S(2)}) collective-permute-start(bf16[256,640]{0,1:T(8,128)(2,1)S(1)} %collective-permute-done.4), channel_id=1, source_target_pairs={{0,7},{1,0},{2,1},{3,2},{4,3},{5,4},{6,5},{7,6},{8,15},{9,8},{10,9... | collective-permute-start | bytes 983048 | tf_op jit(solution)/shard_map/ppermute | solution.py:58
  32.3 7.7 %collective-permute-start.3 = (bf16[256,640]{0,1:T(8,128)(2,1)S(1)}, bf16[256,640]{0,1:T(8,128)(2,1)S(1)}, u32[]{:S(2)}, u32[]{:S(2)}) collective-permute-start(bf16[256,640]{0,1:T(8,128)(2,1)S(1)} %collective-permute-done.2), channel_id=1, source_target_pairs={{0,1},{1,2},{2,3},{3,4},{4,5},{5,6},{6,7},{7,0},{8,9},{9,10},{10,1... | collective-permute-start | bytes 983048 | tf_op jit(solution)/shard_map/ppermute | solution.py:56
  34.8 68.4 %copy-start.2 = (bf16[256,640]{1,0:T(8,128)(2,1)S(1)}, bf16[256,640]{1,0:T(8,128)(2,1)}, u32[]{:S(2)}) copy-start(bf16[256,640]{1,0:T(8,128)(2,1)} %param.9) | copy-start | bytes 983044
  35.5 9.9 %collective-permute-start.6 = (bf16[256,640]{0,1:T(8,128)(2,1)S(1)}, bf16[256,640]{0,1:T(8,128)(2,1)S(1)}, u32[]{:S(2)}, u32[]{:S(2)}) collective-permute-start(bf16[256,640]{0,1:T(8,128)(2,1)S(1)} %collective-permute-done.5), channel_id=1, source_target_pairs={{0,7},{1,0},{2,1},{3,2},{4,3},{5,4},{6,5},{7,6},{8,15},{9,8},{10,9... | collective-permute-start | bytes 983048 | tf_op jit(solution)/shard_map/ppermute | solution.py:58
  52.1 71.0 %copy-start = (bf16[640,2,512]{2,1,0:T(2,128)(2,1)S(1)}, bf16[640,2,512]{2,1,0:T(2,128)(2,1)}, u32[]{:S(2)}) copy-start(bf16[640,2,512]{2,1,0:T(2,128)(2,1)} %param.17) | copy-start | bytes 3932164
  52.1 71.4 %copy-start.5 = (s32[32]{0:T(128)S(1)}, s32[32]{0:T(128)}, u32[]{:S(2)}) copy-start(s32[32]{0:T(128)} %param.13) | copy-start | bytes 388
  123.1 236.3 %reduce-scatter.2.cloned.1.call-start = ((), (), s32[]{:S(2)}) async-start(), calls=%async_computation.3 | async-start | bytes 18874368 | tf_op jit(solution)/shard_map/reduce_scatter | solution.py:85
  267.6 0.9 copy-start.3
  267.6 0.9 copy-start.6
  269.6 93.5 %copy-start.1 = (bf16[16,2,16,128]{3,2,1,0:T(8,128)(2,1)}, bf16[16,2,16,128]{3,2,1,0:T(8,128)(2,1)S(1)}, u32[]{:S(2)}) copy-start(bf16[16,2,16,128]{3,2,1,0:T(8,128)(2,1)S(1)} %scatter_fusion) | copy-start | bytes 393220
Sparse Core Ops, SparseCore 0:
  10.6 92.5 all-gather.2
  123.2 104.0 all-gather.4
  267.7 91.6 reduce-scatter.1
